TPU v7x, 32 devices: a whole 2x2x4 slice. The times are simulated.
32 devices in a mesh: wide: 8 (over y, x, core), narrow: 4 (over z).
Axes of the slice: x: 2, y: 2, z: 4, core: 2. Of those that a mesh axis runs over, the one named last changes fastest.
Arguments:
- states: bfloat16 [16384, 1024], P(('wide', 'narrow')), may hold values from -6 to 6
- applied: bfloat16 [16384, 1024], P(('wide', 'narrow')), may hold values from -6 to 6
- rotation: bfloat16 [2, 1024, 256], P(None, 'wide', 'narrow'), may hold values from -0.1875 to 0.1875
- ritz: float32 [2, 256], replicated, may hold values from 0.5 to 4
- potential: float32 [16384], P(('wide', 'narrow')), may hold values from 0.5 to 8
Outputs:
- rotated: bfloat16 [16384, 2, 256], P(('wide', 'narrow'))
- correction: bfloat16 [16384, 2, 256], P(('wide', 'narrow'))
- margin: float32 [2, 1024, 256], P(None, 'wide', 'narrow')
All inputs are finite; a program needn't handle non-finite values.
Results may differ from a plain program's by a relative error of at most 0.0095.
Values may be sent and summed in bfloat16 or wider, within the bound.
A program may use at most 64 MiB of HBM per device.

v0:
```python
import math
import jax
import jax.numpy as jnp
from jax import lax
from jax.sharding import PartitionSpec as P


def per_device(states, applied, rotation, ritz, potential):
    row_count = states.shape[0]
    total_rows = row_count * lax.axis_size("wide") * lax.axis_size("narrow")
    factor = 1.0 / math.sqrt(total_rows)
    contract = (((0,), (0,)), ((), ()))
    rotated_list = []
    correction_list = []
    margin_list = []
    for window in range(rotation.shape[0]):
        q_local = rotation[window]
        q_tall = lax.all_gather(q_local, "wide", axis=0, tiled=True)
        q_full = lax.all_gather(q_tall, "narrow", axis=1, tiled=True)
        plain = jnp.dot(states, q_full, preferred_element_type=jnp.float32)
        mapped = jnp.dot(applied, q_full, preferred_element_type=jnp.float32)
        eigen_values = ritz[window]
        residual = mapped - plain * eigen_values[None, :]
        fixed = (residual / (potential[:, None] + eigen_values[None, :])).astype(jnp.bfloat16)
        partial_value = lax.psum_scatter(
            lax.dot_general(states, fixed, contract, preferred_element_type=jnp.float32).astype(
                jnp.bfloat16
            ),
            "wide",
            scatter_dimension=0,
            tiled=True,
        )
        summed = lax.psum_scatter(partial_value, "narrow", scatter_dimension=1, tiled=True).astype(
            jnp.float32
        )
        rotated_list.append(plain.astype(jnp.bfloat16))
        correction_list.append(fixed)
        margin_list.append(summed * factor)
    return (
        jnp.stack(rotated_list, axis=1),
        jnp.stack(correction_list, axis=1),
        jnp.stack(margin_list, axis=0),
    )


def solution(mesh):
    placed = (
        P(("wide", "narrow"), None),
        P(("wide", "narrow"), None),
        P(None, "wide", "narrow"),
        P(),
        P(("wide", "narrow")),
    )
    return jax.shard_map(
        per_device,
        mesh=mesh,
        in_specs=placed,
        out_specs=(
            P(("wide", "narrow"), None, None),
            P(("wide", "narrow"), None, None),
            P(None, "wide", "narrow"),
        ),
        check_vma=False,
    )
```

profile of v0, /device:TPU:0, one launch (start us, length us, event | category | flops | bytes accessed | tf_op | source)
XLA Modules:
  0.0 160.5 jit_solution(8119105058409660867)
XLA Ops:
  7.2 0.8 fusion.13
  8.0 0.7 fusion.12
  8.7 10.5 %all-gather.2 = bf16[1,1024,64]{1,2,0:T(8,128)(2,1)S(1)} all-gather(bf16[1,128,64]{1,2,0:T(8,128)(2,1)S(1)} %get-tuple-element.10), channel_id=4, replica_groups=mesh['wide'=8,'narrow'=4] {'wide'}, dimensions={1}, use_global_device_ids=true | all-gather | bytes 147456 | tf_op jit(solution)/shard_map/all_gather | solution.py:18
  19.3 16.3 %all-gather.3 = bf16[1,1024,256]{1,2,0:T(8,128)(2,1)S(1)} all-gather(bf16[1,1024,64]{1,2,0:T(8,128)(2,1)S(1)} %all-gather.2), channel_id=5, replica_groups=mesh['wide'=8,'narrow'=4] {'narrow'}, dimensions={2}, use_global_device_ids=true | all-gather | bytes 655360 | tf_op jit(solution)/shard_map/all_gather | solution.py:19
  35.6 0.5 fusion.7
  36.1 0.7 copy-done.1
  36.8 0.5 fusion.4
  37.3 0.5 fusion.3
  37.8 1.0 copy.14
  38.8 0.0 reduce-scatter.13.cloned.1.call-start
  38.9 9.0 %all-gather = bf16[1,1024,64]{1,2,0:T(8,128)(2,1)S(1)} all-gather(bf16[1,128,64]{1,2,0:T(8,128)(2,1)S(1)} %get-tuple-element.9), channel_id=2, replica_groups=mesh['wide'=8,'narrow'=4] {'wide'}, dimensions={1}, use_global_device_ids=true | all-gather | bytes 147456 | tf_op jit(solution)/shard_map/all_gather | solution.py:18
  47.9 16.6 %all-gather.1 = bf16[1,1024,256]{1,2,0:T(8,128)(2,1)S(1)} all-gather(bf16[1,1024,64]{1,2,0:T(8,128)(2,1)S(1)} %all-gather), channel_id=3, replica_groups=mesh['wide'=8,'narrow'=4] {'narrow'}, dimensions={2}, use_global_device_ids=true | all-gather | bytes 655360 | tf_op jit(solution)/shard_map/all_gather | solution.py:19
  64.5 0.5 fusion.10
  65.0 0.7 copy-done.2
  65.7 0.5 fusion.5
  66.2 0.5 fusion.2
  66.6 1.0 copy.12
  67.7 0.0 reduce-scatter.11.cloned.1.call-start
  67.8 5.8 %reduce-scatter.15.cloned.1.call-done = bf16[128,256]{1,0:T(8,128)(2,1)} async-done(((bf16[1024,256]{1,0:T(8,128)(2,1)}), bf16[128,256]{1,0:T(8,128)(2,1)}) %reduce-scatter.15.cloned.1.call-update) | async-done | bytes 65552
  73.6 1.6 copy.15
  75.2 0.0 reduce-scatter.9.cloned.1.call-start
  75.3 0.1 pad_maximum_fusion
  75.3 1.3 copy.10
  76.7 0.1 pad_maximum_fusion.1
  76.7 1.3 copy.11
  78.0 32.8 %reduce-scatter.13.cloned.1.call-done = bf16[128,256]{1,0:T(8,128)(2,1)} async-done(((bf16[1024,256]{1,0:T(8,128)(2,1)}), bf16[128,256]{1,0:T(8,128)(2,1)}) %reduce-scatter.13.cloned.1.call-update) | async-done | bytes 65552
  110.9 1.6 copy.13
  112.5 20.6 %reduce-scatter.11.cloned.1.call-done = bf16[128,64]{0,1:T(8,128)(2,1)} async-done(((bf16[128,256]{0,1:T(8,128)(2,1)}), bf16[128,64]{0,1:T(8,128)(2,1)}) %reduce-scatter.11.cloned.1.call-update) | async-done | bytes 16400 | tf_op jit(solution)/shard_map/reduce_scatter | solution.py:33
  133.0 0.7 multiply_bitcast_fusion
  133.7 18.9 %reduce-scatter.9.cloned.1.call-done = bf16[128,64]{0,1:T(8,128)(2,1)} async-done(((bf16[128,256]{0,1:T(8,128)(2,1)}), bf16[128,64]{0,1:T(8,128)(2,1)}) %reduce-scatter.9.cloned.1.call-update) | async-done | bytes 16400 | tf_op jit(solution)/shard_map/reduce_scatter | solution.py:33
  152.6 0.7 multiply_bitcast_fusion.1
  153.3 0.6 pad_maximum_fusion.2
  (13 shorter events, 0.2 us)
Async XLA Ops:
  7.2 28.4 %copy-start = (bf16[512,1024]{1,0:T(8,128)(2,1)S(1)}, bf16[512,1024]{1,0:T(8,128)(2,1)}, u32[]{:S(2)}) copy-start(bf16[512,1024]{1,0:T(8,128)(2,1)} %param.5) | copy-start | bytes 3145732
  7.2 66.4 %reduce-scatter.15.cloned.1.call-start = ((), (), s32[]{:S(2)}) async-start(), calls=%async_computation.7 | async-start | bytes 589824
  35.6 1.2 copy-start.1
  36.1 0.7 copy-start.3
  38.8 72.1 %reduce-scatter.13.cloned.1.call-start = ((), (), s32[]{:S(2)}) async-start(), calls=%async_computation.6 | async-start | bytes 589824
  64.5 1.2 copy-start.2
  67.7 65.3 %reduce-scatter.11.cloned.1.call-start = ((), (), s32[]{:S(2)}) async-start(), calls=%async_computation.5 | async-start | bytes 81920 | tf_op jit(solution)/shard_map/reduce_scatter | solution.py:33
  75.2 77.4 %reduce-scatter.9.cloned.1.call-start = ((), (), s32[]{:S(2)}) async-start(), calls=%async_computation.4 | async-start | bytes 81920 | tf_op jit(solution)/shard_map/reduce_scatter | solution.py:33
Sparse Core Ops, SparseCore 0:
  38.9 34.6 reduce-scatter.14
  76.7 34.1 reduce-scatter.12
  113.7 19.2 reduce-scatter.10
  135.1 17.4 reduce-scatter.8
where the time goes:
time: 161 us; the launch traced here: 160 us
  waiting for transfers between devices  78.1 us (49%)
  blocking collectives  52.5 us (33%)
  between operations  13.9 us (9%)
  local copies, waits for them, and re-layouts  10.8 us (7%)
  matrix products  2.82 us (2%)
  other arithmetic  2.24 us (1%)
    reduce_scatter x2, waiting for transfers between devices, per_device(): lax.psum_scatter(partial_value, 'narrow', scatter_dimension=1, tiled=True)  39.4 us
    unnamed x6, waiting for transfers between devices  38.7 us
    all_gather x2, blocking collectives, per_device(): q_full = lax.all_gather(q_tall, 'narrow', axis=1, tiled=True)  32.9 us
    all_gather x2, blocking collectives, per_device(): q_tall = lax.all_gather(q_local, 'wide', axis=0, tiled=True)  19.6 us
    unnamed x14, local copies, waits for them, and re-layouts  9.3 us
  transfers between devices with their start and end apart: 4, of which 4 were waited for; matrix products, arithmetic and copies ran while one was open for 6% of the time, Pallas kernels for 0%

commit v1 on v0

--- a/solution.py
+++ b/solution.py
@@ -3,6 +3,22 @@
 import jax.numpy as jnp
 from jax import lax
 from jax.sharding import PartitionSpec as P
+
+
+def ring_gather(x, axis, dim):
+    ways, here, lap = (lax.axis_size(axis), lax.axis_index(axis), x.shape[dim])
+    shape = [n * ways if d == dim else n for d, n in enumerate(x.shape)]
+    full = lax.dynamic_update_slice_in_dim(jnp.zeros(shape, x.dtype), x, here * lap, axis=dim)
+    going_up = going_down = x
+    for far in range(1, ways // 2 + 1):
+        going_up = lax.ppermute(going_up, axis, [(d, (d + 1) % ways) for d in range(ways)])
+        full = lax.dynamic_update_slice_in_dim(full, going_up, (here - far) % ways * lap, axis=dim)
+        if 2 * far < ways:
+            going_down = lax.ppermute(going_down, axis, [(d, (d - 1) % ways) for d in range(ways)])
+            full = lax.dynamic_update_slice_in_dim(
+                full, going_down, (here + far) % ways * lap, axis=dim
+            )
+    return full
 
 
 def per_device(states, applied, rotation, ritz, potential):
@@ -15,7 +31,7 @@
     margin_list = []
     for window in range(rotation.shape[0]):
         q_local = rotation[window]
-        q_tall = lax.all_gather(q_local, "wide", axis=0, tiled=True)
+        q_tall = ring_gather(q_local, "wide", 0)
         q_full = lax.all_gather(q_tall, "narrow", axis=1, tiled=True)
         plain = jnp.dot(states, q_full, preferred_element_type=jnp.float32)
         mapped = jnp.dot(applied, q_full, preferred_element_type=jnp.float32)

time: 161 us -> 187 us (1.16)
  waiting for transfers between devices: 78.1 us -> 105 us
  blocking collectives: 52.5 us -> 33.2 us
  starting transfers between devices: 0.16 us -> 16.8 us
    unnamed x6, waiting for transfers between devices: 38.7 us -> 61.6 us
    all_gather x2 -> x0, blocking collectives: 19.6 us -> none  [per_device(): q_tall = lax.all_gather(q_local, 'wide', axis=0, tiled=True)]
    ppermute x0 -> x14, starting transfers between devices: none -> 16.7 us  [the longest x6 16.1 us: ring_gather(): lax.ppermute(going_down, axis, [(d, (d - 1) % ways) for d in range(ways)])]
    ppermute x0 -> x14, waiting for transfers between devices: none -> 3.99 us  [the longest x8 3.97 us: ring_gather(): lax.ppermute(going_up, axis, [(d, (d + 1) % ways) for d in range(ways)])]
    unnamed x14 -> x22, local copies, waits for them, and re-layouts: 9.3 us -> 10.9 us
  transfers between devices with their start and end apart: 4 -> 18, of which waited for: 4 -> 6; matrix products, arithmetic and copies ran while one was open for 6% -> 5% of each run, Pallas kernels for 0% -> 0%
where the time goes in v1:
time: 187 us; the launch traced here: 186 us
  waiting for transfers between devices  105 us (56%)
  blocking collectives  33.2 us (18%)
  starting transfers between devices  16.8 us (9%)
  between operations  14 us (7%)
  local copies, waits for them, and re-layouts  12 us (6%)
  matrix products  2.8 us (1%)
  other arithmetic  2.25 us (1%)
    unnamed x6, waiting for transfers between devices  61.6 us
    reduce_scatter x2, waiting for transfers between devices, per_device(): lax.psum_scatter(partial_value, 'narrow', scatter_dimension=1, tiled=True)  39.3 us
    all_gather x2, blocking collectives, per_device(): q_full = lax.all_gather(q_tall, 'narrow', axis=1, tiled=True)  33.2 us
    ppermute x6, starting transfers between devices, ring_gather(): lax.ppermute(going_down, axis, [(d, (d - 1) % ways) for d in range(ways)])  16.1 us
    unnamed x22, local copies, waits for them, and re-layouts  10.9 us
    ppermute x8, waiting for transfers between devices, ring_gather(): lax.ppermute(going_up, axis, [(d, (d + 1) % ways) for d in range(ways)])  3.97 us
  transfers between devices with their start and end apart: 18, of which 6 were waited for; matrix products, arithmetic and copies ran while one was open for 5% of the time, Pallas kernels for 0%

profile of v1, /device:TPU:0, one launch (start us, length us, event | category | flops | bytes accessed | tf_op | source)
XLA Modules:
  0.0 186.0 jit_solution(13667729301216434335)
XLA Ops:
  7.2 0.8 slice_bitcast_fusion.1
  8.0 0.5 collective-permute-start
  8.5 2.9 %collective-permute-start.1 = (bf16[128,64]{0,1:T(8,128)(2,1)S(1)}, bf16[128,64]{0,1:T(8,128)(2,1)S(1)}, u32[]{:S(2)}, u32[]{:S(2)}) collective-permute-start(bf16[128,64]{0,1:T(8,128)(2,1)S(1)} %get-tuple-element.9), channel_id=1, source_target_pairs={{0,28},{4,0},{8,4},{12,8},{16,12},{20,16},{24,20},{28,24},{1,29},{... | collective-permute-start | bytes 49160 | tf_op jit(solution)/shard_map/ppermute | solution.py:17
  11.4 2.6 %collective-permute-start.8 = (bf16[128,64]{0,1:T(8,128)(2,1)S(1)}, bf16[128,64]{0,1:T(8,128)(2,1)S(1)}, u32[]{:S(2)}, u32[]{:S(2)}) collective-permute-start(bf16[128,64]{0,1:T(8,128)(2,1)S(1)} %get-tuple-element.10), channel_id=1, source_target_pairs={{0,28},{4,0},{8,4},{12,8},{16,12},{20,16},{24,20},{28,24},{1,29},{... | collective-permute-start | bytes 49160 | tf_op jit(solution)/shard_map/ppermute | solution.py:17
  14.1 0.7 copy-done.3
  14.9 0.7 copy-done.4
  15.5 2.6 %collective-permute-start.3 = (bf16[128,64]{0,1:T(8,128)(2,1)S(1)}, bf16[128,64]{0,1:T(8,128)(2,1)S(1)}, u32[]{:S(2)}, u32[]{:S(2)}) collective-permute-start(bf16[128,64]{0,1:T(8,128)(2,1)S(1)} %collective-permute-done.1), channel_id=1, source_target_pairs={{0,28},{4,0},{8,4},{12,8},{16,12},{20,16},{24,20},{28,24},{1,29},{... | collective-permute-start | bytes 49160 | tf_op jit(solution)/shard_map/ppermute | solution.py:17
  18.2 2.6 %collective-permute-start.10 = (bf16[128,64]{0,1:T(8,128)(2,1)S(1)}, bf16[128,64]{0,1:T(8,128)(2,1)S(1)}, u32[]{:S(2)}, u32[]{:S(2)}) collective-permute-start(bf16[128,64]{0,1:T(8,128)(2,1)S(1)} %collective-permute-done.8), channel_id=1, source_target_pairs={{0,28},{4,0},{8,4},{12,8},{16,12},{20,16},{24,20},{28,24},{1,29},{... | collective-permute-start | bytes 49160 | tf_op jit(solution)/shard_map/ppermute | solution.py:17
  21.0 2.6 %collective-permute-start.5 = (bf16[128,64]{0,1:T(8,128)(2,1)S(1)}, bf16[128,64]{0,1:T(8,128)(2,1)S(1)}, u32[]{:S(2)}, u32[]{:S(2)}) collective-permute-start(bf16[128,64]{0,1:T(8,128)(2,1)S(1)} %collective-permute-done.3), channel_id=1, source_target_pairs={{0,28},{4,0},{8,4},{12,8},{16,12},{20,16},{24,20},{28,24},{1,29},{... | collective-permute-start | bytes 49160 | tf_op jit(solution)/shard_map/ppermute | solution.py:17
  23.6 2.6 %collective-permute-start.12 = (bf16[128,64]{0,1:T(8,128)(2,1)S(1)}, bf16[128,64]{0,1:T(8,128)(2,1)S(1)}, u32[]{:S(2)}, u32[]{:S(2)}) collective-permute-start(bf16[128,64]{0,1:T(8,128)(2,1)S(1)} %collective-permute-done.10), channel_id=1, source_target_pairs={{0,28},{4,0},{8,4},{12,8},{16,12},{20,16},{24,20},{28,24},{1,29},{... | collective-permute-start | bytes 49160 | tf_op jit(solution)/shard_map/ppermute | solution.py:17
  26.4 1.3 collective-permute-done.11
  27.8 2.7 %collective-permute-done.6 = bf16[128,64]{0,1:T(8,128)(2,1)S(1)} collective-permute-done((bf16[128,64]{0,1:T(8,128)(2,1)S(1)}, bf16[128,64]{0,1:T(8,128)(2,1)S(1)}, u32[]{:S(2)}, u32[]{:S(2)}) %collective-permute-start.6) | collective-permute-done | bytes 16416 | tf_op jit(solution)/shard_map/ppermute | solution.py:14
  30.4 17.2 %all_gather.6 = bf16[1024,256]{0,1:T(8,128)(2,1)S(1)} all-gather(bf16[1024,64]{0,1:T(8,128)(2,1)S(1)} %constant_dynamic-update-slice_fusion.8), channel_id=1, replica_groups=mesh['wide'=8,'narrow'=4] {'narrow'}, dimensions={1}, use_global_device_ids=true | all-gather | bytes 655360 | tf_op jit(solution)/shard_map/all_gather | solution.py:35
  47.6 16.1 %all_gather.7 = bf16[1024,256]{0,1:T(8,128)(2,1)S(1)} all-gather(bf16[1024,64]{0,1:T(8,128)(2,1)S(1)} %constant_dynamic-update-slice_fusion), channel_id=1, replica_groups=mesh['wide'=8,'narrow'=4] {'narrow'}, dimensions={1}, use_global_device_ids=true | all-gather | bytes 655360 | tf_op jit(solution)/shard_map/all_gather | solution.py:35
  64.2 0.7 copy-done.5
  64.9 0.5 fusion.7
  65.9 1.0 copy.12
  67.4 0.7 copy-done.6
  68.2 0.5 fusion.6
  68.7 0.7 copy-done.1
  69.8 1.0 copy.14
  71.0 28.3 %reduce-scatter.13.cloned.1.call-done = bf16[128,256]{1,0:T(8,128)(2,1)} async-done(((bf16[1024,256]{1,0:T(8,128)(2,1)}), bf16[128,256]{1,0:T(8,128)(2,1)}) %reduce-scatter.13.cloned.1.call-update) | async-done | bytes 65552
  99.2 1.6 copy.13
  101.0 1.1 copy.10
  102.1 1.1 copy.11
  103.2 33.3 %reduce-scatter.15.cloned.1.call-done = bf16[128,256]{1,0:T(8,128)(2,1)} async-done(((bf16[1024,256]{1,0:T(8,128)(2,1)}), bf16[128,256]{1,0:T(8,128)(2,1)}) %reduce-scatter.15.cloned.1.call-update) | async-done | bytes 65552
  136.5 1.6 copy.15
  138.1 20.0 %reduce-scatter.9.cloned.1.call-done = bf16[128,64]{0,1:T(8,128)(2,1)} async-done(((bf16[128,256]{0,1:T(8,128)(2,1)}), bf16[128,64]{0,1:T(8,128)(2,1)}) %reduce-scatter.9.cloned.1.call-update) | async-done | bytes 16400 | tf_op jit(solution)/shard_map/reduce_scatter | solution.py:49
  158.0 0.7 multiply_bitcast_fusion.1
  158.8 19.4 %reduce-scatter.11.cloned.1.call-done = bf16[128,64]{0,1:T(8,128)(2,1)} async-done(((bf16[128,256]{0,1:T(8,128)(2,1)}), bf16[128,64]{0,1:T(8,128)(2,1)}) %reduce-scatter.11.cloned.1.call-update) | async-done | bytes 16400 | tf_op jit(solution)/shard_map/reduce_scatter | solution.py:49
  178.1 0.7 multiply_bitcast_fusion
  178.9 0.6 pad_maximum_fusion.2
  (65 shorter events, 2.6 us)
Async XLA Ops:
  7.2 56.5 %copy-start = (bf16[512,1024]{1,0:T(8,128)(2,1)S(1)}, bf16[512,1024]{1,0:T(8,128)(2,1)}, u32[]{:S(2)}) copy-start(bf16[512,1024]{1,0:T(8,128)(2,1)} %param.5) | copy-start | bytes 3145732
  7.2 92.1 %reduce-scatter.13.cloned.1.call-start = ((), (), s32[]{:S(2)}) async-start(), calls=%async_computation.6 | async-start | bytes 589824
  8.0 7.5 %collective-permute-start = (bf16[128,64]{0,1:T(8,128)(2,1)S(1)}, bf16[128,64]{0,1:T(8,128)(2,1)S(1)}, u32[]{:S(2)}, u32[]{:S(2)}) collective-permute-start(bf16[128,64]{0,1:T(8,128)(2,1)S(1)} %get-tuple-element.9), channel_id=1, source_target_pairs={{0,4},{4,8},{8,12},{12,16},{16,20},{20,24},{24,28},{28,0},{1,5},{5... | collective-permute-start | bytes 49160 | tf_op jit(solution)/shard_map/ppermute | solution.py:14
  8.5 7.0 %collective-permute-start.1 = (bf16[128,64]{0,1:T(8,128)(2,1)S(1)}, bf16[128,64]{0,1:T(8,128)(2,1)S(1)}, u32[]{:S(2)}, u32[]{:S(2)}) collective-permute-start(bf16[128,64]{0,1:T(8,128)(2,1)S(1)} %get-tuple-element.9), channel_id=1, source_target_pairs={{0,28},{4,0},{8,4},{12,8},{16,12},{20,16},{24,20},{28,24},{1,29},{... | collective-permute-start | bytes 49160 | tf_op jit(solution)/shard_map/ppermute | solution.py:17
  11.4 6.8 %collective-permute-start.7 = (bf16[128,64]{0,1:T(8,128)(2,1)S(1)}, bf16[128,64]{0,1:T(8,128)(2,1)S(1)}, u32[]{:S(2)}, u32[]{:S(2)}) collective-permute-start(bf16[128,64]{0,1:T(8,128)(2,1)S(1)} %get-tuple-element.10), channel_id=1, source_target_pairs={{0,4},{4,8},{8,12},{12,16},{16,20},{20,24},{24,28},{28,0},{1,5},{5... | collective-permute-start | bytes 49160 | tf_op jit(solution)/shard_map/ppermute | solution.py:14
  11.4 6.8 %collective-permute-start.8 = (bf16[128,64]{0,1:T(8,128)(2,1)S(1)}, bf16[128,64]{0,1:T(8,128)(2,1)S(1)}, u32[]{:S(2)}, u32[]{:S(2)}) collective-permute-start(bf16[128,64]{0,1:T(8,128)(2,1)S(1)} %get-tuple-element.10), channel_id=1, source_target_pairs={{0,28},{4,0},{8,4},{12,8},{16,12},{20,16},{24,20},{28,24},{1,29},{... | collective-permute-start | bytes 49160 | tf_op jit(solution)/shard_map/ppermute | solution.py:17
  14.1 0.8 copy-start.3
  14.8 0.7 copy-start.4
  15.5 5.4 %collective-permute-start.2 = (bf16[128,64]{0,1:T(8,128)(2,1)S(1)}, bf16[128,64]{0,1:T(8,128)(2,1)S(1)}, u32[]{:S(2)}, u32[]{:S(2)}) collective-permute-start(bf16[128,64]{0,1:T(8,128)(2,1)S(1)} %collective-permute-done), channel_id=1, source_target_pairs={{0,4},{4,8},{8,12},{12,16},{16,20},{20,24},{24,28},{28,0},{1,5},{5... | collective-permute-start | bytes 49160 | tf_op jit(solution)/shard_map/ppermute | solution.py:14
  15.5 5.4 %collective-permute-start.3 = (bf16[128,64]{0,1:T(8,128)(2,1)S(1)}, bf16[128,64]{0,1:T(8,128)(2,1)S(1)}, u32[]{:S(2)}, u32[]{:S(2)}) collective-permute-start(bf16[128,64]{0,1:T(8,128)(2,1)S(1)} %collective-permute-done.1), channel_id=1, source_target_pairs={{0,28},{4,0},{8,4},{12,8},{16,12},{20,16},{24,20},{28,24},{1,29},{... | collective-permute-start | bytes 49160 | tf_op jit(solution)/shard_map/ppermute | solution.py:17
  18.2 5.4 %collective-permute-start.9 = (bf16[128,64]{0,1:T(8,128)(2,1)S(1)}, bf16[128,64]{0,1:T(8,128)(2,1)S(1)}, u32[]{:S(2)}, u32[]{:S(2)}) collective-permute-start(bf16[128,64]{0,1:T(8,128)(2,1)S(1)} %collective-permute-done.7), channel_id=1, source_target_pairs={{0,4},{4,8},{8,12},{12,16},{16,20},{20,24},{24,28},{28,0},{1,5},{5... | collective-permute-start | bytes 49160 | tf_op jit(solution)/shard_map/ppermute | solution.py:14
  18.2 5.4 %collective-permute-start.10 = (bf16[128,64]{0,1:T(8,128)(2,1)S(1)}, bf16[128,64]{0,1:T(8,128)(2,1)S(1)}, u32[]{:S(2)}, u32[]{:S(2)}) collective-permute-start(bf16[128,64]{0,1:T(8,128)(2,1)S(1)} %collective-permute-done.8), channel_id=1, source_target_pairs={{0,28},{4,0},{8,4},{12,8},{16,12},{20,16},{24,20},{28,24},{1,29},{... | collective-permute-start | bytes 49160 | tf_op jit(solution)/shard_map/ppermute | solution.py:17
  20.9 5.4 %collective-permute-start.4 = (bf16[128,64]{0,1:T(8,128)(2,1)S(1)}, bf16[128,64]{0,1:T(8,128)(2,1)S(1)}, u32[]{:S(2)}, u32[]{:S(2)}) collective-permute-start(bf16[128,64]{0,1:T(8,128)(2,1)S(1)} %collective-permute-done.2), channel_id=1, source_target_pairs={{0,4},{4,8},{8,12},{12,16},{16,20},{20,24},{24,28},{28,0},{1,5},{5... | collective-permute-start | bytes 49160 | tf_op jit(solution)/shard_map/ppermute | solution.py:14
  21.0 6.8 %collective-permute-start.5 = (bf16[128,64]{0,1:T(8,128)(2,1)S(1)}, bf16[128,64]{0,1:T(8,128)(2,1)S(1)}, u32[]{:S(2)}, u32[]{:S(2)}) collective-permute-start(bf16[128,64]{0,1:T(8,128)(2,1)S(1)} %collective-permute-done.3), channel_id=1, source_target_pairs={{0,28},{4,0},{8,4},{12,8},{16,12},{20,16},{24,20},{28,24},{1,29},{... | collective-permute-start | bytes 49160 | tf_op jit(solution)/shard_map/ppermute | solution.py:17
  23.6 4.1 %collective-permute-start.11 = (bf16[128,64]{0,1:T(8,128)(2,1)S(1)}, bf16[128,64]{0,1:T(8,128)(2,1)S(1)}, u32[]{:S(2)}, u32[]{:S(2)}) collective-permute-start(bf16[128,64]{0,1:T(8,128)(2,1)S(1)} %collective-permute-done.9), channel_id=1, source_target_pairs={{0,4},{4,8},{8,12},{12,16},{16,20},{20,24},{24,28},{28,0},{1,5},{5... | collective-permute-start | bytes 49160 | tf_op jit(solution)/shard_map/ppermute | solution.py:14
  23.6 4.1 %collective-permute-start.12 = (bf16[128,64]{0,1:T(8,128)(2,1)S(1)}, bf16[128,64]{0,1:T(8,128)(2,1)S(1)}, u32[]{:S(2)}, u32[]{:S(2)}) collective-permute-start(bf16[128,64]{0,1:T(8,128)(2,1)S(1)} %collective-permute-done.10), channel_id=1, source_target_pairs={{0,28},{4,0},{8,4},{12,8},{16,12},{20,16},{24,20},{28,24},{1,29},{... | collective-permute-start | bytes 49160 | tf_op jit(solution)/shard_map/ppermute | solution.py:17
  26.3 4.1 %collective-permute-start.6 = (bf16[128,64]{0,1:T(8,128)(2,1)S(1)}, bf16[128,64]{0,1:T(8,128)(2,1)S(1)}, u32[]{:S(2)}, u32[]{:S(2)}) collective-permute-start(bf16[128,64]{0,1:T(8,128)(2,1)S(1)} %collective-permute-done.4), channel_id=1, source_target_pairs={{0,4},{4,8},{8,12},{12,16},{16,20},{20,24},{24,28},{28,0},{1,5},{5... | collective-permute-start | bytes 49160 | tf_op jit(solution)/shard_map/ppermute | solution.py:14
  27.7 19.9 %collective-permute-start.13 = (bf16[128,64]{0,1:T(8,128)(2,1)S(1)}, bf16[128,64]{0,1:T(8,128)(2,1)S(1)}, u32[]{:S(2)}, u32[]{:S(2)}) collective-permute-start(bf16[128,64]{0,1:T(8,128)(2,1)S(1)} %collective-permute-done.11), channel_id=1, source_target_pairs={{0,4},{4,8},{8,12},{12,16},{16,20},{20,24},{24,28},{28,0},{1,5},{5... | collective-permute-start | bytes 49160 | tf_op jit(solution)/shard_map/ppermute | solution.py:14
  63.7 1.2 copy-start.5
  64.2 0.7 copy-start.7
  66.9 69.6 %reduce-scatter.15.cloned.1.call-start = ((), (), s32[]{:S(2)}) async-start(), calls=%async_computation.7 | async-start | bytes 589824
  66.9 1.2 copy-start.6
  68.7 0.7 copy-start.1
  70.9 87.2 %reduce-scatter.9.cloned.1.call-start = ((), (), s32[]{:S(2)}) async-start(), calls=%async_computation.4 | async-start | bytes 81920 | tf_op jit(solution)/shard_map/reduce_scatter | solution.py:49
  100.8 77.3 %reduce-scatter.11.cloned.1.call-start = ((), (), s32[]{:S(2)}) async-start(), calls=%async_computation.5 | async-start | bytes 81920 | tf_op jit(solution)/shard_map/reduce_scatter | solution.py:49
  100.9 1.1 copy-start.2
Sparse Core Ops, SparseCore 0:
  67.0 32.1 reduce-scatter.12
  102.3 34.1 reduce-scatter.14
  138.7 19.2 reduce-scatter.8
  160.7 17.3 reduce-scatter.10
